TPU v7x, 32 devices: a whole 2x2x4 slice. The times are simulated.
32 devices in a mesh: ctx: 8 (over z, x), head: 4 (over y, core).
Axes of the slice: x: 2, y: 2, z: 4, core: 2. Of those that a mesh axis runs over, the one named last changes fastest.
Arguments:
- query_in: bfloat16 [1024, 8192], P('ctx', 'head'), may hold values from -6 to 6
- key_in: bfloat16 [1024, 8192], P('ctx', 'head'), may hold values from -6 to 6
- value_in: bfloat16 [1024, 8192], P('ctx', 'head'), may hold values from -12 to 12
- conv_taps: float32 [3, 4, 8192], P(None, None, 'head'), may hold values from -3 to 3
- norm_gain: float32 [8192], P('head'), may hold values from 0.25 to 1.75
- cotangent: bfloat16 [1024, 8192], P('ctx', 'head'), may hold values from -6 to 6
Outputs:
- attended: bfloat16 [1024, 8192], P('ctx', 'head')
- grad_query: bfloat16 [1024, 8192], P('ctx', 'head')
- grad_key: bfloat16 [1024, 8192], P('ctx', 'head')
- grad_value: bfloat16 [1024, 8192], P('ctx', 'head')
- grad_taps: float32 [3, 4, 8192], P(None, None, 'head')
- grad_gain: float32 [8192], P('head')
All inputs are finite; a program needn't handle non-finite values.
Results may differ from a plain program's by a relative error of at most 0.0074.
Values may be sent and summed in bfloat16 or wider, within the bound.
A program may use at most 192 MiB of HBM per device.

v0:
```python
import math

import jax
import jax.numpy as jnp
from jax import lax
from jax.sharding import PartitionSpec as P

DH = 128
W = 8192
KS = 4


epsilon = 1e-06


def from_behind(block, axis, distance):
    devices = range(lax.axis_size(axis))
    route = [(i - distance, i) for i in devices if i - distance in devices]
    return lax.ppermute(block, axis, route)


def prefix(part, axis, combine, identity, reverse):
    count = lax.axis_size(axis)
    place = lax.axis_index(axis)
    ahead = count - 1 - place if reverse else place
    gathered = lax.all_gather(part, axis)
    state = jnp.zeros_like(part) + jnp.asarray(identity, part.dtype)

    def one(turn, state):
        source = count - 1 - turn if reverse else turn
        return combine(state, lax.dynamic_index_in_dim(gathered, source, 0, False))

    return lax.fori_loop(0, ahead, one, state)


def conv_rows(padded, taps):
    row_count = padded.shape[0] - (KS - 1)
    summed = jnp.zeros((row_count, padded.shape[1]), jnp.float32)
    for offset in range(KS):
        summed = summed + taps[offset] * padded[offset : offset + row_count].astype(jnp.float32)
    return summed


def conv_back(extended, taps):
    row_count = extended.shape[0] - (KS - 1)
    summed = jnp.zeros((row_count, extended.shape[1]), jnp.float32)
    for offset in range(KS):
        first_row = KS - 1 - offset
        summed = summed + taps[offset] * extended[first_row : first_row + row_count]
    return summed


def taps_grad(gradient, padded):
    row_count = gradient.shape[0]
    return jnp.stack(
        [
            jnp.sum(gradient * padded[offset : offset + row_count].astype(jnp.float32), axis=0)
            for offset in range(KS)
        ]
    )


def silu_slope(preact):
    sigmoid_val = jax.nn.sigmoid(preact)
    return sigmoid_val * (1.0 + preact * (1.0 - sigmoid_val))


def as_heads(source):
    return source.reshape(source.shape[0], source.shape[1] // DH, DH)


def add_states(earlier_part, later_part):
    return earlier_part + later_part


def shards(query_in, key_in, value_in, conv_taps, norm_gain, cotangent):
    row_count = query_in.shape[0]
    channels = query_in.shape[1]
    edge_rows = KS - 1
    devices = lax.axis_size("ctx")
    tails = jnp.stack(
        [
            query_in[row_count - edge_rows :],
            key_in[row_count - edge_rows :],
            value_in[row_count - edge_rows :],
        ]
    )
    before = from_behind(tails, "ctx", 1)
    padded = [
        jnp.concatenate([before[member], source], axis=0)
        for member, source in enumerate((query_in, key_in, value_in))
    ]
    pre_query = conv_rows(padded[0], conv_taps[0])
    pre_key = conv_rows(padded[1], conv_taps[1])
    pre_value = conv_rows(padded[2], conv_taps[2])
    query_heads = as_heads(jax.nn.silu(pre_query).astype(jnp.bfloat16))
    key_heads = as_heads(jax.nn.silu(pre_key).astype(jnp.bfloat16))
    value_heads = as_heads(pre_value.astype(jnp.bfloat16))
    local_state = jnp.einsum(
        "thd,the->hde", key_heads, value_heads, preferred_element_type=jnp.float32
    )
    earlier = prefix(local_state, "ctx", add_states, jnp.zeros_like(local_state), False)
    earlier_b = earlier.astype(jnp.bfloat16)
    causal = jnp.arange(row_count)[:, None] >= jnp.arange(row_count)[None, :]
    scores = jnp.einsum("thd,shd->hts", query_heads, key_heads, preferred_element_type=jnp.float32)
    weights_b = jnp.where(causal[None], scores, 0.0).astype(jnp.bfloat16)
    within = jnp.einsum("hts,shd->thd", weights_b, value_heads, preferred_element_type=jnp.float32)
    carried = jnp.einsum("thd,hde->the", query_heads, earlier_b, preferred_element_type=jnp.float32)
    mixed = (within + carried).reshape(row_count, channels)
    square_sum = lax.psum(jnp.sum(mixed * mixed, axis=1), "head")
    inverse = lax.rsqrt(square_sum / W + epsilon)[:, None]
    attended = (mixed * inverse * norm_gain).astype(jnp.bfloat16)
    grad_up = cotangent.astype(jnp.float32)
    scaled = norm_gain * grad_up
    dotted = (lax.psum(jnp.sum(scaled * mixed, axis=1), "head") / W)[:, None]
    grad_mixed = (inverse * scaled - mixed * inverse**3 * dotted).astype(jnp.bfloat16)
    gain_local = jnp.sum(grad_up * mixed * inverse, axis=0)
    grad_heads = as_heads(grad_mixed)
    query_state = jnp.einsum(
        "thd,the->hde", query_heads, grad_heads, preferred_element_type=jnp.float32
    )
    later_sum = prefix(query_state, "ctx", add_states, jnp.zeros_like(query_state), True)
    later_b = later_sum.astype(jnp.bfloat16)
    grad_scores = jnp.einsum(
        "the,she->hts", grad_heads, value_heads, preferred_element_type=jnp.float32
    )
    grad_weights = jnp.where(causal[None], grad_scores, 0.0).astype(jnp.bfloat16)
    grad_qf = jnp.einsum(
        "hts,shd->thd", grad_weights, key_heads, preferred_element_type=jnp.float32
    ) + jnp.einsum("the,hde->thd", grad_heads, earlier_b, preferred_element_type=jnp.float32)
    grad_kf = jnp.einsum(
        "hts,thd->shd", grad_weights, query_heads, preferred_element_type=jnp.float32
    ) + jnp.einsum("she,hde->shd", value_heads, later_b, preferred_element_type=jnp.float32)
    grad_vf = jnp.einsum(
        "hts,the->she", weights_b, grad_heads, preferred_element_type=jnp.float32
    ) + jnp.einsum("shd,hde->she", key_heads, later_b, preferred_element_type=jnp.float32)
    grads_pre = [
        grad_qf.reshape(row_count, channels) * silu_slope(pre_query),
        grad_kf.reshape(row_count, channels) * silu_slope(pre_key),
        grad_vf.reshape(row_count, channels),
    ]
    leading = jnp.stack([gradient[:edge_rows] for gradient in grads_pre])
    ahead_rows = from_behind(leading, "ctx", -1)
    grads_in = []
    taps_parts = []
    for member in range(3):
        extended = jnp.concatenate([grads_pre[member], ahead_rows[member]], axis=0)
        grads_in.append(conv_back(extended, conv_taps[member]).astype(jnp.bfloat16))
        taps_parts.append(taps_grad(grads_pre[member], padded[member]))
    taps_total, gain_total = lax.psum((jnp.stack(taps_parts), gain_local), "ctx")
    scale = 1.0 / math.sqrt(row_count * devices)
    return (attended, grads_in[0], grads_in[1], grads_in[2], taps_total * scale, gain_total * scale)


def solution(mesh):
    placed = (
        P("ctx", "head"),
        P("ctx", "head"),
        P("ctx", "head"),
        P(None, None, "head"),
        P("head"),
        P("ctx", "head"),
    )
    return jax.shard_map(
        shards,
        mesh=mesh,
        in_specs=placed,
        out_specs=(
            P("ctx", "head"),
            P("ctx", "head"),
            P("ctx", "head"),
            P("ctx", "head"),
            P(None, None, "head"),
            P("head"),
        ),
        check_vma=False,
    )
```

profile of v0, /device:TPU:0, one launch (start us, length us, event | category | flops | bytes accessed | tf_op | source)
XLA Modules:
  0.0 410.4 jit_solution(17114481659029187848)
XLA Ops:
  7.2 0.8 slice_bitcast_fusion.10
  8.0 0.8 slice_bitcast_fusion.8
  8.8 4.9 %collective-permute-start = (bf16[3,3,2048]{2,1,0:T(4,128)(2,1)S(1)}, bf16[3,3,2048]{2,1,0:T(4,128)(2,1)S(1)}, u32[]{:S(2)}, u32[]{:S(2)}) collective-permute-start(bf16[3,3,2048]{2,1,0:T(4,128)(2,1)S(1)} %pad_maximum_fusion.8), channel_id=1, source_target_pairs={{0,4},{4,8},{8,12},{12,16},{16,20},{20,24},{24,28},{1,5},{5,9},{9,... | collective-permute-start | bytes 110600 | tf_op jit(solution)/shard_map/ppermute | solution.py:19
  13.7 1.1 fusion.84
  14.9 0.6 collective-permute-done
  15.5 2.6 fusion.103
  18.1 0.1 copy.80
  18.2 0.5 copy.46
  18.8 0.4 copy-done.9
  19.1 0.5 fusion.65
  19.7 1.4 fusion.72
  21.1 0.0 all-gather.7.cloned.1.call-start
  21.2 0.7 multiply_convert_fusion.2
  21.9 0.3 copy.76
  22.2 0.7 fusion.104
  22.9 0.5 fusion
  23.4 0.8 copy-done.13
  24.2 0.5 fusion.68
  24.7 123.1 %all-gather.5.cloned.1.call-done = f32[128,128,128]{2,1,0:T(8,128)} async-done(((f32[16,128,128]{2,1,0:T(8,128)}), f32[128,128,128]{2,1,0:T(8,128)}) %all-gather.5.cloned.1.call-update) | async-done | bytes 8388624 | tf_op jit(solution)/shard_map/all_gather | solution.py:26
  147.8 0.1 broadcast_in_dim.27.clone
  147.9 1.4 fusion.58
  149.4 1.6 copy.50
  151.0 5.9 %psum.28 = f32[128]{0:T(128)S(1)} all-reduce(f32[128]{0:T(128)S(1)} %get-tuple-element.142), channel_id=1, replica_groups=mesh['ctx'=8,'head'=4] {'head'}, use_global_device_ids=true, to_apply=%region_3.4 | all-reduce | flops 128 | bytes 1024 | tf_op jit(solution)/shard_map/psum | solution.py:110
  156.8 1.4 fusion.54
  158.2 6.4 %psum.29 = f32[128]{0:T(128)S(1)} all-reduce(f32[128]{0:T(128)S(1)} %get-tuple-element.97), channel_id=1, replica_groups=mesh['ctx'=8,'head'=4] {'head'}, use_global_device_ids=true, to_apply=%region_5.6 | all-reduce | flops 128 | bytes 1024 | tf_op jit(solution)/shard_map/psum | solution.py:115
  164.6 2.6 fusion.29
  167.3 1.3 copy.77
  168.6 1.5 fusion.87
  170.1 0.0 all-reduce.2.cloned.1.call-start
  170.1 0.5 fusion.1
  170.6 0.4 copy-done.3
  171.1 0.5 fusion.85
  171.5 1.4 convolution_add_fusion.2
  172.9 1.6 copy.57
  174.5 31.1 %psum.31 = f32[2048]{0:T(1024)S(1)} all-reduce(f32[2048]{0:T(1024)S(1)} %get-tuple-element.96), channel_id=1, replica_groups=mesh['ctx'=8,'head'=4] {'ctx'}, use_global_device_ids=true, to_apply=%region_22.23 | all-reduce | flops 2048 | bytes 16384 | tf_op jit(solution)/shard_map/psum | solution.py:150
  205.7 0.6 broadcast_multiply_fusion.1
  206.3 1.3 fusion.42
  207.7 1.3 fusion.88
  209.0 0.1 copy-done.16
  209.1 1.3 fusion.86
  210.4 93.1 %all-gather.7.cloned.1.call-done = f32[128,128,128]{2,1,0:T(8,128)} async-done(((f32[16,128,128]{2,1,0:T(8,128)}), f32[128,128,128]{2,1,0:T(8,128)}) %all-gather.7.cloned.1.call-update) | async-done | bytes 8388624 | tf_op jit(solution)/shard_map/all_gather | solution.py:26
  303.4 0.1 broadcast_in_dim.27
  303.5 10.8 %while.23 = (s32[]{:T(128)}, f32[16,128,128]{2,1,0:T(8,128)S(1)}, s32[]{:T(128)}, f32[8,16,128,128]{3,2,1,0:T(8,128)}, s32[]{:T(128)}, /*index=5*/s32[]{:T(128)}, s32[]{:T(128)}, s32[]{:T(128)}) while((s32[]{:T(128)}, f32[16,128,128]{2,1,0:T(8,128)S(1)}, s32[]{:T(128)}, f32[8,16,128,128]{3,2,1,0:T(8,128)}, s32[]{:T(128)}, ...), condition=%wide.region_7.8_spmd, body=%wide.region_6.7_spmd.sunk | while | flops 262150 | bytes 3145871 | solution.py:33
  303.6 1.5 bitcast_add_fusion.5
  305.1 1.5 bitcast_add_fusion.5
  306.6 1.5 bitcast_add_fusion.5
  308.1 1.5 bitcast_add_fusion.5
  309.7 1.5 bitcast_add_fusion.5
  311.2 1.5 bitcast_add_fusion.5
  312.7 1.5 bitcast_add_fusion.5
  314.4 1.7 convolution_add_fusion
  316.1 0.3 copy.66
  316.4 2.7 convolution_add_fusion.1
  319.1 2.6 copy.62
  321.7 2.4 fusion.49
  324.2 1.3 collective-permute-start.1
  325.5 1.3 copy.67
  326.9 3.8 collective-permute-done.1
  330.7 1.3 fusion.25
  332.0 1.9 fusion.35
  334.0 0.7 pad_maximum_fusion.7
  334.7 1.3 fusion.17
  336.0 66.3 %all-reduce.2.cloned.1.call-done = f32[3,4,2048]{2,1,0:T(4,128)} async-done(((f32[3,4,2048]{2,1,0:T(4,128)}), f32[3,4,2048]{2,1,0:T(4,128)}) %all-reduce.2.cloned.1.call-update) | async-done | bytes 98320 | tf_op jit(solution)/shard_map/psum | solution.py:150
  402.3 1.6 broadcast_multiply_fusion
  (65 shorter events, 0.5 us)
Async XLA Ops:
  7.2 140.7 %all-gather.5.cloned.1.call-start = ((), (), s32[]{:S(2)}) async-start(), calls=%async_computation.1 | async-start | bytes 9437184 | tf_op jit(solution)/shard_map/all_gather | solution.py:26
  8.8 6.6 %collective-permute-start = (bf16[3,3,2048]{2,1,0:T(4,128)(2,1)S(1)}, bf16[3,3,2048]{2,1,0:T(4,128)(2,1)S(1)}, u32[]{:S(2)}, u32[]{:S(2)}) collective-permute-start(bf16[3,3,2048]{2,1,0:T(4,128)(2,1)S(1)} %pad_maximum_fusion.8), channel_id=1, source_target_pairs={{0,4},{4,8},{8,12},{12,16},{16,20},{20,24},{24,28},{1,5},{5,9},{9,... | collective-permute-start | bytes 110600 | tf_op jit(solution)/shard_map/ppermute | solution.py:19
  14.8 3.9 copy-start.17
  14.8 3.9 copy-start.19
  14.8 3.9 copy-start.21
  14.8 3.9 copy-start.23
  18.1 1.0 copy-start.9
  18.7 2.4 copy-start.2
  19.7 1.5 copy-start.7
  21.1 1.1 copy-start
  21.1 282.3 %all-gather.7.cloned.1.call-start = ((), (), s32[]{:S(2)}) async-start(), calls=%async_computation.2 | async-start | bytes 9437184 | tf_op jit(solution)/shard_map/all_gather | solution.py:26
  22.9 1.8 copy-start.11
  23.4 0.8 copy-start.13
  149.4 7.4 %copy-start.25 = (f32[2048]{0:T(1024)S(1)}, f32[2048]{0:T(1024)}, u32[]{:S(2)}) copy-start(f32[2048]{0:T(1024)} %param.14) | copy-start | bytes 24580
  170.0 1.0 copy-start.3
  170.1 232.2 %all-reduce.2.cloned.1.call-start = ((), (), s32[]{:S(2)}) async-start(), calls=%async_computation | async-start | bytes 196608 | tf_op jit(solution)/shard_map/psum | solution.py:150
  171.1 1.8 copy-start.15
  172.9 33.4 %copy-start.8 = (bf16[128,2048]{1,0:T(8,128)(2,1)S(1)}, bf16[128,2048]{1,0:T(8,128)(2,1)}, u32[]{:S(2)}) copy-start(bf16[128,2048]{1,0:T(8,128)(2,1)} %param.10) | copy-start | bytes 1572868
  206.3 1.4 copy-start.14
  207.6 2.7 copy-start.4
  207.6 1.4 copy-start.16
  303.5 10.8 %copy-start.12 = (bf16[16,16,8,128]{3,2,1,0:T(8,128)(2,1)S(1)}, bf16[16,16,8,128]{3,2,1,0:T(8,128)(2,1)}, u32[]{:S(2)}) copy-start(bf16[16,16,8,128]{3,2,1,0:T(8,128)(2,1)} %copy-done.11) | copy-start | bytes 1572868
  319.1 2.6 copy-start.1
  324.2 6.5 %collective-permute-start.1 = (f32[3,3,2048]{2,1,0:T(4,128)S(1)}, f32[3,3,2048]{2,1,0:T(4,128)S(1)}, u32[]{:S(2)}, u32[]{:S(2)}) collective-permute-start(f32[3,3,2048]{2,1,0:T(4,128)S(1)} %pad_maximum_fusion.6), channel_id=1, source_target_pairs={{4,0},{8,4},{12,8},{16,12},{20,16},{24,20},{28,24},{5,1},{9,5},{13... | collective-permute-start | bytes 221192 | tf_op jit(solution)/shard_map/ppermute | solution.py:19
  325.5 5.2 %copy-start.5 = (f32[128,2048]{1,0:T(8,128)S(1)}, f32[128,2048]{1,0:T(8,128)}, u32[]{:S(2)}) copy-start(f32[128,2048]{1,0:T(8,128)} %copy-done.4) | copy-start | bytes 3145732
  326.9 5.1 %copy-start.6 = (f32[128,2048]{1,0:T(8,128)S(1)}, f32[128,2048]{1,0:T(8,128)}, u32[]{:S(2)}) copy-start(f32[128,2048]{1,0:T(8,128)} %copy.67) | copy-start | bytes 3145732
  326.9 5.1 %copy-start.10 = (bf16[128,2048]{1,0:T(8,128)(2,1)S(1)}, bf16[128,2048]{1,0:T(8,128)(2,1)}, u32[]{:S(2)}) copy-start(bf16[128,2048]{1,0:T(8,128)(2,1)} %param.12) | copy-start | bytes 1572868
  326.9 5.1 %copy-start.18 = (f32[1,1,2048]{2,1,0:T(1,128)S(1)}, f32[1,1,2048]{2,1,0:T(1,128)}, u32[]{:S(2)}) copy-start(f32[1,1,2048]{2,1,0:T(1,128)} %copy-done.17) | copy-start | bytes 24580
  326.9 5.1 %copy-start.20 = (f32[1,1,2048]{2,1,0:T(1,128)S(1)}, f32[1,1,2048]{2,1,0:T(1,128)}, u32[]{:S(2)}) copy-start(f32[1,1,2048]{2,1,0:T(1,128)} %copy-done.19) | copy-start | bytes 24580
  326.9 5.1 %copy-start.22 = (f32[1,1,2048]{2,1,0:T(1,128)S(1)}, f32[1,1,2048]{2,1,0:T(1,128)}, u32[]{:S(2)}) copy-start(f32[1,1,2048]{2,1,0:T(1,128)} %copy-done.21) | copy-start | bytes 24580
  326.9 5.1 %copy-start.24 = (f32[1,1,2048]{2,1,0:T(1,128)S(1)}, f32[1,1,2048]{2,1,0:T(1,128)}, u32[]{:S(2)}) copy-start(f32[1,1,2048]{2,1,0:T(1,128)} %copy-done.23) | copy-start | bytes 24580
Sparse Core Ops, SparseCore 0:
  21.2 126.5 all-gather.4
  170.2 133.2 all-gather.6
  334.8 67.4 all-reduce.1
where the time goes:
time: 412 us; the launch traced here: 410 us
  waiting for transfers between devices  287 us (70%)
  blocking collectives  43.4 us (11%)
  other arithmetic  30.3 us (7%)
  matrix products  14.6 us (4%)
  local copies, waits for them, and re-layouts  14.3 us (3%)
  between operations  14.2 us (3%)
  starting transfers between devices  6.29 us (2%)
    all_gather x2, waiting for transfers between devices, prefix(): gathered = lax.all_gather(part, axis)  216 us
    psum x1, waiting for transfers between devices, shards(): lax.psum((jnp.stack(taps_parts), gain_local), 'ctx')  66.3 us
    psum x1, blocking collectives, shards(): lax.psum((jnp.stack(taps_parts), gain_local), 'ctx')  31.1 us
    add x7, other arithmetic, add_states(): return earlier_part + later_part  10.5 us
  transfers between devices with their start and end apart: 5, of which 5 were waited for; matrix products, arithmetic and copies ran while one was open for 4% of the time, Pallas kernels for 0%

commit v1 on v0

v1 whole, which is shorter than its diff:
```python
import functools
import math

import jax
import jax.numpy as jnp
from jax import lax
from jax.experimental import pallas as pl
from jax.experimental.pallas import tpu as pltpu
from jax.sharding import PartitionSpec as P

DH = 128
W = 8192
KS = 4
GROUP = 2
TAIL = 8
EPSILON = 1e-06

f32 = jnp.float32
bf16 = jnp.bfloat16
MESH = pl.DeviceIdType.MESH


def dot(a, b, da, db):
    return lax.dot_general(a, b, (((da,), (db,)), ((), ())), preferred_element_type=f32)


def kernel(n_ctx, n_head, heads, *refs):
    (q_ref, k_ref, v_ref, taps_ref, gain_ref, g_ref,
     att_ref, gq_ref, gk_ref, gv_ref, gt_ref, gg_ref,
     tails, slope_q, slope_k, qf, kf, vf, gm, pb, sb, own, mixed, d0, dk, dv,
     acc_sq, acc_dot, inv_b, coef_b,
     u_out, u_in, t_out, t_in, w_out, w_in, r_out, r_in,
     lead_q, lead_q_in, lead_kv, lead_kv_in,
     part_a, part_b, rs_a, rs_b, own_a, own_b, ag_a, ag_b, stat, stat_in,
     s_tail, r_tail, s_u, r_u, s_t, r_t, s_w, r_w, s_r, r_r,
     s_lead, r_lead, s_stat, r_stat, s_rsa, r_rsa, s_rsb, r_rsb,
     s_aga, r_aga, s_agb, r_agb) = refs
    rows = q_ref.shape[0]
    width = heads * DH
    chunks = heads // GROUP
    pairs = n_ctx // 2
    me = lax.axis_index("ctx")
    head_me = lax.axis_index("head")
    pair = lax.div(me, 2)
    minor = lax.rem(me, 2)
    partner = pair * 2 + 1 - minor
    is_odd = minor.astype(f32)
    is_even = 1.0 - is_odd
    owners = min(n_ctx, width // 128)
    piece = width // owners

    barrier = pltpu.get_barrier_semaphore()

    def greet(i, _):
        pl.semaphore_signal(barrier, inc=1, device_id={"ctx": lax.rem(me + i, n_ctx)}, device_id_type=MESH)
        return 0

    lax.fori_loop(1, n_ctx, greet, 0)
    for i in range(1, n_head):
        pl.semaphore_signal(barrier, inc=1, device_id={"head": lax.rem(head_me + i, n_head)}, device_id_type=MESH)

    @pl.when(me == 0)
    def _():
        tails[...] = jnp.zeros_like(tails)

    @pl.when(me == n_ctx - 1)
    def _():
        lead_q_in[...] = jnp.zeros_like(lead_q_in)
        lead_kv_in[...] = jnp.zeros_like(lead_kv_in)

    @pl.when(pair == 0)
    def _():
        t_in[...] = jnp.zeros_like(t_in)

    @pl.when(pair == pairs - 1)
    def _():
        r_in[...] = jnp.zeros_like(r_in)

    part_a[...] = jnp.zeros_like(part_a)
    acc_sq[...] = jnp.zeros_like(acc_sq)
    acc_dot[...] = jnp.zeros_like(acc_dot)

    pl.semaphore_wait(barrier, n_ctx - 1 + n_head - 1)

    def send(src, dst, ssem, rsem, ctx):
        return pltpu.make_async_remote_copy(
            src_ref=src, dst_ref=dst, send_sem=ssem, recv_sem=rsem,
            device_id={"ctx": ctx}, device_id_type=MESH)

    following = lax.rem(me + 1, n_ctx)
    previous = lax.rem(me + n_ctx - 1, n_ctx)
    next_pair = lax.rem(me + 2, n_ctx)
    last_pair = lax.rem(me + n_ctx - 2, n_ctx)

    inputs = (q_ref, k_ref, v_ref)

    def tail_copy(m):
        return send(inputs[m].at[pl.ds(rows - TAIL, TAIL), :], tails.at[m], s_tail.at[m], r_tail.at[m], following)

    @pl.when(me < n_ctx - 1)
    def _():
        for m in range(3):
            tail_copy(m).start()

    @pl.when(me > 0)
    def _():
        for m in range(3):
            tail_copy(m).wait_recv()

    def lanes_of(h):
        return pl.ds(pl.multiple_of(h * DH, DH), DH)

    def shifted(m, lanes):
        ext = jnp.concatenate(
            [tails[m, :, lanes].astype(f32)[TAIL - 8:], inputs[m][:, lanes].astype(f32)], axis=0)
        return [ext[8 - (KS - 1) + j: 8 - (KS - 1) + j + rows] for j in range(KS)]

    def conv(m, lanes):
        xs = shifted(m, lanes)
        total = taps_ref[m, 0:1, lanes] * xs[0]
        for j in range(1, KS):
            total = total + taps_ref[m, j:j + 1, lanes] * xs[j]
        return total

    def taps_grad(m, lanes, d):
        return [jnp.sum(d * x, axis=0, keepdims=True) for x in shifted(m, lanes)]

    row_ids = lax.broadcasted_iota(jnp.int32, (rows, rows), 0)
    col_ids = lax.broadcasted_iota(jnp.int32, (rows, rows), 1)
    causal = row_ids >= col_ids

    def u_copy(c):
        return send(u_out.at[c], u_in.at[c], s_u.at[c], r_u.at[c], partner)

    def t_copy(c):
        return send(t_out.at[c], t_in.at[c], s_t.at[c], r_t.at[c], next_pair)

    def w_copy(c):
        return send(w_out.at[c], w_in.at[c], s_w.at[c], r_w.at[c], partner)

    def r_copy(c):
        return send(r_out.at[c], r_in.at[c], s_r.at[c], r_r.at[c], last_pair)

    def features(c, _):
        for i in range(GROUP):
            h = c * GROUP + i
            lanes = lanes_of(h)
            pre = conv(1, lanes)
            sig = 1.0 / (1.0 + jnp.exp(-pre))
            slope_k[:, lanes] = sig * (1.0 + pre * (1.0 - sig))
            kb = (pre * sig).astype(bf16)
            kf[:, lanes] = kb
            vb = conv(2, lanes).astype(bf16)
            vf[:, lanes] = vb
            state = dot(kb, vb, 0, 0)
            own[h] = state
            u_out[c, i] = state.astype(bf16)
        u_copy(c).start()
        return 0

    lax.fori_loop(0, chunks, features, 0)

    def within(c, _):
        for i in range(GROUP):
            h = c * GROUP + i
            lanes = lanes_of(h)
            pre = conv(0, lanes)
            sig = 1.0 / (1.0 + jnp.exp(-pre))
            slope_q[:, lanes] = sig * (1.0 + pre * (1.0 - sig))
            qb = (pre * sig).astype(bf16)
            qf[:, lanes] = qb
            weights = jnp.where(causal, dot(qb, kf[:, lanes], 1, 1), 0.0).astype(bf16)
            pb[h] = weights
            mixed[:, lanes] = dot(weights, vf[:, lanes], 1, 0)
        return 0

    lax.fori_loop(0, chunks, within, 0)

    def carried(c, _):
        u_copy(c).wait_recv()

        @pl.when(pair > 0)
        def _():
            t_copy(c).wait_recv()

        @pl.when(pair < pairs - 1)
        def _():
            for i in range(GROUP):
                t_out[c, i] = (t_in[c, i].astype(f32) + (u_in[c, i].astype(f32) + own[c * GROUP + i])).astype(t_out.dtype)
            t_copy(c).start()

        for i in range(GROUP):
            h = c * GROUP + i
            lanes = lanes_of(h)
            state = (t_in[c, i].astype(f32) + is_odd * u_in[c, i].astype(f32)).astype(bf16)
            sb[h] = state
            mix = mixed[:, lanes] + dot(qf[:, lanes], state, 1, 0)
            mixed[:, lanes] = mix
            acc_sq[...] += mix * mix
            acc_dot[...] += (gain_ref[:, lanes] * g_ref[:, lanes].astype(f32)) * mix
        return 0

    lax.fori_loop(0, chunks, carried, 0)

    stat[0:1, :] = jnp.sum(acc_sq[...].T, axis=0, keepdims=True)
    stat[1:2, :] = jnp.sum(acc_dot[...].T, axis=0, keepdims=True)
    stat[2:8, :] = jnp.zeros((6, rows), f32)

    def stat_copy(i):
        return pltpu.make_async_remote_copy(
            src_ref=stat, dst_ref=stat_in.at[i], send_sem=s_stat.at[i], recv_sem=r_stat.at[i],
            device_id={"head": lax.rem(head_me + i + 1, n_head)}, device_id_type=MESH)

    for i in range(n_head - 1):
        stat_copy(i).start()
    for i in range(n_head - 1):
        stat_copy(i).wait_recv()
    total = stat[...]
    for i in range(n_head - 1):
        total = total + stat_in[i]
    mean_sq = jnp.broadcast_to(total[0:1], (rows, rows)).T / W
    mean_dot = jnp.broadcast_to(total[1:2], (rows, rows)).T / W
    inverse = lax.rsqrt(mean_sq + EPSILON)
    inv_b[...] = inverse
    coef_b[...] = inverse * inverse * inverse * mean_dot

    def norm(c, _):
        for i in range(GROUP):
            h = c * GROUP + i
            lanes = lanes_of(h)
            mix = mixed[:, lanes]
            inv = inv_b[...]
            gain = gain_ref[:, lanes]
            up = g_ref[:, lanes].astype(f32)
            normed = mix * inv
            att_ref[:, lanes] = (normed * gain).astype(bf16)
            gmb = (inv * (gain * up) - mix * coef_b[...]).astype(bf16)
            gm[:, lanes] = gmb
            part_a[4:5, lanes] = jnp.sum(up * normed, axis=0, keepdims=True)
            state = dot(qf[:, lanes], gmb, 0, 0)
            own[h] = state
            w_out[c, i] = state.astype(bf16)
        w_copy(c).start()
        return 0

    lax.fori_loop(0, chunks, norm, 0)

    def local_grads(c, _):
        for i in range(GROUP):
            h = c * GROUP + i
            lanes = lanes_of(h)
            gmb = gm[:, lanes]
            dp = jnp.where(causal, dot(gmb, vf[:, lanes], 1, 1), 0.0).astype(bf16)
            dq = dot(dp, kf[:, lanes], 1, 0) + dot(gmb, sb[h], 1, 1)
            dq = dq * slope_q[:, lanes]
            d0[:, lanes] = dq
            lead_q[:, lanes] = dq[:8]
            for j, row in enumerate(taps_grad(0, lanes, dq)):
                part_a[j:j + 1, lanes] = row
            dk[:, lanes] = dot(dp, qf[:, lanes], 0, 0)
            dv[:, lanes] = dot(pb[h], gmb, 0, 0)
        return 0

    lax.fori_loop(0, chunks, local_grads, 0)

    def lead_copy(i):
        src, dst = ((lead_q, lead_q_in), (lead_kv, lead_kv_in))[i]
        return send(src, dst, s_lead.at[i], r_lead.at[i], previous)

    @pl.when(me > 0)
    def _():
        lead_copy(0).start()

    def span(o):
        return pl.ds(pl.multiple_of(o * piece, 128), piece)

    def rs_copy(i, part, held, ssem, rsem):
        to = lax.rem(me + i, n_ctx)
        return to, send(part.at[:, span(lax.rem(to, owners))], held.at[i], ssem.at[i], rsem.at[i], to)

    def rs_start(part, held, ssem, rsem):
        def one(i, _):
            to, copy = rs_copy(i, part, held, ssem, rsem)

            @pl.when(to < owners)
            def _():
                copy.start()
            return 0

        lax.fori_loop(1, n_ctx, one, 0)

    def ag_copy(i, mine, ag, ssem, rsem):
        to = lax.rem(me + i, n_ctx)
        return send(mine, ag.at[:, span(lax.rem(me, owners))], ssem.at[i], rsem.at[i], to)

    def rs_finish(part, held, ssem, rsem, mine, ag, ag_ssem, ag_rsem):
        @pl.when(me < owners)
        def _():
            mine[...] = part[:, span(me)]

            def one(i, _):
                rs_copy(i, part, held, ssem, rsem)[1].wait_recv()
                mine[...] += held[i]
                return 0

            lax.fori_loop(1, n_ctx, one, 0)

            def out(i, _):
                ag_copy(i, mine, ag, ag_ssem, ag_rsem).start()
                return 0

            lax.fori_loop(1, n_ctx, out, 0)
            ag[:, span(me)] = mine[...]

    def ag_finish(part, held, ssem, rsem, mine, ag, ag_ssem, ag_rsem):
        def one(i, _):
            @pl.when(lax.rem(me - i + n_ctx, n_ctx) < owners)
            def _():
                ag_copy(i, mine, ag, ag_ssem, ag_rsem).wait_recv()

            @pl.when(me < owners)
            def _():
                ag_copy(i, mine, ag, ag_ssem, ag_rsem).wait_send()

            @pl.when(lax.rem(me + i, n_ctx) < owners)
            def _():
                rs_copy(i, part, held, ssem, rsem)[1].wait_send()
            return 0

        lax.fori_loop(1, n_ctx, one, 0)

    set_a = (part_a, rs_a, s_rsa, r_rsa, own_a, ag_a, s_aga, r_aga)
    set_b = (part_b, rs_b, s_rsb, r_rsb, own_b, ag_b, s_agb, r_agb)
    rs_start(*set_a[:4])

    def state_grads(turn, _):
        c = turn
        w_copy(c).wait_recv()

        @pl.when(pair < pairs - 1)
        def _():
            r_copy(c).wait_recv()

        @pl.when(pair > 0)
        def _():
            for i in range(GROUP):
                r_out[c, i] = (r_in[c, i].astype(f32) + (w_in[c, i].astype(f32) + own[c * GROUP + i])).astype(r_out.dtype)
            r_copy(c).start()

        for i in range(GROUP):
            h = c * GROUP + i
            lanes = lanes_of(h)
            state = (r_in[c, i].astype(f32) + is_even * w_in[c, i].astype(f32)).astype(bf16)
            d1 = (dk[:, lanes] + dot(vf[:, lanes], state, 1, 1)) * slope_k[:, lanes]
            d2 = dv[:, lanes] + dot(kf[:, lanes], state, 1, 0)
            dk[:, lanes] = d1
            dv[:, lanes] = d2
            lead_kv[0, :, lanes] = d1[:8]
            lead_kv[1, :, lanes] = d2[:8]
            for m, d in ((1, d1), (2, d2)):
                for j, row in enumerate(taps_grad(m, lanes, d)):
                    part_b[(m - 1) * KS + j:(m - 1) * KS + j + 1, lanes] = row
        return 0

    lax.fori_loop(0, chunks, state_grads, 0)

    @pl.when(me > 0)
    def _():
        lead_copy(1).start()

    rs_start(*set_b[:4])
    rs_finish(*set_a)

    def conv_back(m, d_ref, lanes, ahead, out_ref):
        ext = jnp.concatenate([d_ref[:, lanes], ahead], axis=0)
        summed = taps_ref[m, 0:1, lanes] * ext[KS - 1:KS - 1 + rows]
        for j in range(1, KS):
            summed = summed + taps_ref[m, j:j + 1, lanes] * ext[KS - 1 - j:KS - 1 - j + rows]
        out_ref[:, lanes] = summed.astype(bf16)

    @pl.when(me < n_ctx - 1)
    def _():
        lead_copy(0).wait_recv()

    def back_q(h, _):
        lanes = lanes_of(h)
        conv_back(0, d0, lanes, lead_q_in[:, lanes], gq_ref)
        return 0

    lax.fori_loop(0, heads, back_q, 0)
    rs_finish(*set_b)

    @pl.when(me < n_ctx - 1)
    def _():
        lead_copy(1).wait_recv()

    def back_kv(h, _):
        lanes = lanes_of(h)
        conv_back(1, dk, lanes, lead_kv_in[0, :, lanes], gk_ref)
        conv_back(2, dv, lanes, lead_kv_in[1, :, lanes], gv_ref)
        return 0

    lax.fori_loop(0, heads, back_kv, 0)

    @pl.when(me < n_ctx - 1)
    def _():
        for m in range(3):
            tail_copy(m).wait_send()

    @pl.when(me > 0)
    def _():
        lead_copy(0).wait_send()
        lead_copy(1).wait_send()

    for i in range(n_head - 1):
        stat_copy(i).wait_send()

    def drain(c, _):
        u_copy(c).wait_send()
        w_copy(c).wait_send()

        @pl.when(pair < pairs - 1)
        def _():
            t_copy(c).wait_send()

        @pl.when(pair > 0)
        def _():
            r_copy(c).wait_send()
        return 0

    lax.fori_loop(0, chunks, drain, 0)
    ag_finish(*set_a)
    ag_finish(*set_b)
    scale = 1.0 / math.sqrt(rows * n_ctx)
    gt_ref[0] = ag_a[0:4, :] * scale
    gg_ref[...] = ag_a[4:5, :] * scale
    gt_ref[1] = ag_b[0:4, :] * scale
    gt_ref[2] = ag_b[4:8, :] * scale


def shards(n_ctx, n_head, query_in, key_in, value_in, conv_taps, norm_gain, cotangent):
    rows, width = query_in.shape
    heads = width // DH
    chunks = heads // GROUP
    owners = min(n_ctx, width // 128)
    piece = width // owners
    chain = bf16 if n_ctx <= 16 else f32
    vm = pltpu.VMEM
    dma = pltpu.SemaphoreType.DMA
    tile = (rows, width)
    states = (chunks, GROUP, DH, DH)
    scratch = [
        vm((3, TAIL, width), bf16), vm(tile, f32), vm(tile, f32),
        vm(tile, bf16), vm(tile, bf16), vm(tile, bf16), vm(tile, bf16),
        vm((heads, rows, rows), bf16), vm((heads, DH, DH), bf16), vm((heads, DH, DH), f32),
        vm(tile, f32), vm(tile, f32), vm(tile, f32), vm(tile, f32),
        vm((rows, DH), f32), vm((rows, DH), f32), vm((rows, rows), f32), vm((rows, rows), f32),
        vm(states, bf16), vm(states, bf16), vm(states, chain), vm(states, chain),
        vm(states, bf16), vm(states, bf16), vm(states, chain), vm(states, chain),
        vm((8, width), f32), vm((8, width), f32), vm((2, 8, width), f32), vm((2, 8, width), f32),
        vm((8, width), f32), vm((8, width), f32),
        vm((n_ctx, 8, piece), f32), vm((n_ctx, 8, piece), f32),
        vm((8, piece), f32), vm((8, piece), f32),
        vm((8, width), f32), vm((8, width), f32),
        vm((8, rows), f32), vm((n_head - 1, 8, rows), f32),
        dma((3,)), dma((3,)),
        dma((chunks,)), dma((chunks,)), dma((chunks,)), dma((chunks,)),
        dma((chunks,)), dma((chunks,)), dma((chunks,)), dma((chunks,)),
        dma((2,)), dma((2,)), dma((n_head - 1,)), dma((n_head - 1,)),
        dma((n_ctx,)), dma((n_ctx,)), dma((n_ctx,)), dma((n_ctx,)),
        dma((n_ctx,)), dma((n_ctx,)), dma((n_ctx,)), dma((n_ctx,)),
    ]
    block = pl.BlockSpec(memory_space=pltpu.VMEM)
    att, gq, gk, gv, gt, gg = pl.pallas_call(
        functools.partial(kernel, n_ctx, n_head, heads),
        out_shape=(
            jax.ShapeDtypeStruct(tile, bf16),
            jax.ShapeDtypeStruct(tile, bf16),
            jax.ShapeDtypeStruct(tile, bf16),
            jax.ShapeDtypeStruct(tile, bf16),
            jax.ShapeDtypeStruct((3, KS, width), f32),
            jax.ShapeDtypeStruct((1, width), f32),
        ),
        in_specs=[block] * 6,
        out_specs=(block,) * 6,
        scratch_shapes=scratch,
        compiler_params=pltpu.CompilerParams(
            collective_id=0, has_side_effects=True, vmem_limit_bytes=48 * 1024 * 1024),
        name="attend",
    )(query_in, key_in, value_in, conv_taps, norm_gain.reshape(1, width), cotangent)
    return att, gq, gk, gv, gt, gg.reshape(width)


def solution(mesh):
    tokens = P("ctx", "head")
    placed = (tokens, tokens, tokens, P(None, None, "head"), P("head"), tokens)
    return jax.shard_map(
        functools.partial(shards, mesh.shape["ctx"], mesh.shape["head"]),
        mesh=mesh,
        in_specs=placed,
        out_specs=(tokens, tokens, tokens, tokens, P(None, None, "head"), P("head")),
        check_vma=False,
    )
```

time: 412 us -> 90.2 us (0.22)
  waiting for transfers between devices: 287 us -> 0 us
  Pallas kernels: 0 us -> 79 us
  blocking collectives: 43.4 us -> 0 us
  other arithmetic: 30.3 us -> 0 us
  matrix products: 14.6 us -> 0 us
  between operations: 14.2 us -> 0.66 us
  starting transfers between devices: 6.29 us -> 0 us
    all_gather x2 -> x0, waiting for transfers between devices: 216 us -> none  [prefix(): gathered = lax.all_gather(part, axis)]
    pallas_call x0 -> x1, Pallas kernels: none -> 79 us  [shards(): pl.pallas_call(functools.partial(kernel, n_ctx, n_head, heads), out_shape...]
    psum x1 -> x0, waiting for transfers between devices: 66.3 us -> none  [shards(): lax.psum((jnp.stack(taps_parts), gain_local), 'ctx')]
    psum x3 -> x0, blocking collectives: 43.4 us -> none  [the longest x1 31.1 us: shards(): lax.psum((jnp.stack(taps_parts), gain_local), 'ctx')]
    dot_general x12 -> x0, matrix products: 14.6 us -> none  [the longest x1 2.7 us: shards(): jnp.einsum('she,hde->shd', value_heads, later_b, preferred_element_type=j...]
    add x7 -> x0, other arithmetic: 10.5 us -> none  [add_states(): return earlier_part + later_part]
    reshape x7 -> x0, local copies, waits for them, and re-layouts: 9.15 us -> none  [the longest x1 2.59 us: shards(): grad_kf.reshape(row_count, channels) * silu_slope(pre_key)]
    unnamed x53 -> x18, local copies, waits for them, and re-layouts: 1.94 us -> 10.2 us
  transfers between devices with their start and end apart: 5 -> 0, of which waited for: 5 -> 0; matrix products, arithmetic and copies ran while one was open for 4% -> 0% of each run, Pallas kernels for 0% -> 0%
where the time goes in v1:
time: 90.2 us; the launch traced here: 89.8 us
  Pallas kernels  79 us (88%)
  local copies, waits for them, and re-layouts  10.2 us (11%)
    pallas_call x1, Pallas kernels, shards(): pl.pallas_call(functools.partial(kernel, n_ctx, n_head, heads), out_shape...  79 us
    unnamed x18, local copies, waits for them, and re-layouts  10.2 us

profile of v1, /device:TPU:0, one launch (start us, length us, event | category | flops | bytes accessed | tf_op | source)
XLA Modules:
  0.0 89.8 jit_solution(262920901065309447)
XLA Ops:
  0.6 0.0 copy-start
  0.6 1.0 %copy-done = bf16[128,2048]{1,0:T(8,128)(2,1)S(1)} copy-done((bf16[128,2048]{1,0:T(8,128)(2,1)S(1)}, bf16[128,2048]{1,0:T(8,128)(2,1)}, u32[]{:S(2)}) %copy-start) | copy-done | bytes 524312
  1.7 0.0 copy-start.1
  1.7 1.0 %copy-done.1 = bf16[128,2048]{1,0:T(8,128)(2,1)S(1)} copy-done((bf16[128,2048]{1,0:T(8,128)(2,1)S(1)}, bf16[128,2048]{1,0:T(8,128)(2,1)}, u32[]{:S(2)}) %copy-start.1) | copy-done | bytes 524312
  2.7 0.0 copy-start.2
  2.7 1.0 %copy-done.2 = bf16[128,2048]{1,0:T(8,128)(2,1)S(1)} copy-done((bf16[128,2048]{1,0:T(8,128)(2,1)S(1)}, bf16[128,2048]{1,0:T(8,128)(2,1)}, u32[]{:S(2)}) %copy-start.2) | copy-done | bytes 524312
  3.8 0.0 copy-start.3
  3.8 1.0 %copy-done.3 = bf16[128,2048]{1,0:T(8,128)(2,1)S(1)} copy-done((bf16[128,2048]{1,0:T(8,128)(2,1)S(1)}, bf16[128,2048]{1,0:T(8,128)(2,1)}, u32[]{:S(2)}) %copy-start.3) | copy-done | bytes 524312
  4.8 0.0 copy-start.4
  4.8 0.9 copy-done.4
  5.7 0.0 copy-start.5
  5.7 0.7 copy-done.5
  6.4 79.0 %attend.1 = (bf16[128,2048]{1,0:T(8,128)(2,1)S(1)}, bf16[128,2048]{1,0:T(8,128)(2,1)S(1)}, bf16[128,2048]{1,0:T(8,128)(2,1)S(1)}, bf16[128,2048]{1,0:T(8,128)(2,...) custom-call(bf16[128,2048]{1,0:T(8,128)(2,1)S(1)} %copy-done, bf16[128,2048]{1,0:T(8,128)(2,1)S(1)} %copy-done.1, ...), custom_call_target="tpu_custom_call" | custom-call | tf_op jit(solution)/shard_map/attend/pallas_call | solution.py:474
  85.4 0.8 copy.18
  86.2 0.8 copy.19
  87.0 0.8 copy.20
  87.8 0.8 copy.21
  88.6 0.6 copy.22
  89.2 0.6 copy.23
Async XLA Ops:
  0.6 1.0 %copy-start = (bf16[128,2048]{1,0:T(8,128)(2,1)S(1)}, bf16[128,2048]{1,0:T(8,128)(2,1)}, u32[]{:S(2)}) copy-start(bf16[128,2048]{1,0:T(8,128)(2,1)} %refs_0_.1) | copy-start | bytes 1572868
  1.7 1.0 %copy-start.1 = (bf16[128,2048]{1,0:T(8,128)(2,1)S(1)}, bf16[128,2048]{1,0:T(8,128)(2,1)}, u32[]{:S(2)}) copy-start(bf16[128,2048]{1,0:T(8,128)(2,1)} %refs_1_.1) | copy-start | bytes 1572868
  2.7 1.0 %copy-start.2 = (bf16[128,2048]{1,0:T(8,128)(2,1)S(1)}, bf16[128,2048]{1,0:T(8,128)(2,1)}, u32[]{:S(2)}) copy-start(bf16[128,2048]{1,0:T(8,128)(2,1)} %refs_2_.1) | copy-start | bytes 1572868
  3.8 1.0 %copy-start.3 = (bf16[128,2048]{1,0:T(8,128)(2,1)S(1)}, bf16[128,2048]{1,0:T(8,128)(2,1)}, u32[]{:S(2)}) copy-start(bf16[128,2048]{1,0:T(8,128)(2,1)} %refs_5_.1) | copy-start | bytes 1572868
  4.8 0.9 copy-start.4
  5.7 0.7 copy-start.5
